TPU v7x, 32 devices: a whole 2x2x4 slice. The times are simulated.
32 devices in a mesh: rep: 4 (over z), fsdp: 8 (over y, x, core).
Axes of the slice: x: 2, y: 2, z: 4, core: 2. Of those that a mesh axis runs over, the one named last changes fastest.
Arguments:
- tokens: bfloat16 [4, 2048, 1024], P('rep', 'fsdp'), may hold values from -6 to 6
- segment_ids: int32 [4, 2048], P('rep'), may hold values from 0 to 7, never falling along the last dimension, each value on 1 to 1280 neighbouring positions
- qkv_weight: bfloat16 [1024, 3072], P('fsdp'), may hold values from -0.1875 to 0.1875
- out_weight: bfloat16 [1024, 1024], P('fsdp'), may hold values from -1.5 to 1.5
- up_weight: bfloat16 [1024, 4096], P('fsdp'), may hold values from -0.1875 to 0.1875
- down_weight: bfloat16 [4096, 1024], P('fsdp'), may hold values from -0.09375 to 0.09375
- proj_bias: float32 [4, 1024], replicated, may hold values from -1.2 to 1.2
- hidden_bias: float32 [4096], replicated, may hold values from -1.2 to 1.2
- norm_gain: float32 [2, 1024], replicated, may hold values from 0.5 to 1.5
- norm_shift: float32 [2, 1024], replicated, may hold values from -1.2 to 1.2
- cotangent: bfloat16 [4, 2048, 1024], P('rep', 'fsdp'), may hold values from -6 to 6
Outputs:
- output: bfloat16 [4, 2048, 1024], P('rep', 'fsdp')
- input_grad: bfloat16 [4, 2048, 1024], P('rep', 'fsdp')
- qkv_grad: float32 [1024, 3072], P('fsdp')
- out_grad: float32 [1024, 1024], P('fsdp')
- up_grad: float32 [1024, 4096], P('fsdp')
- down_grad: float32 [4096, 1024], P('fsdp')
- proj_bias_grad: float32 [4, 1024], replicated
- hidden_bias_grad: float32 [4096], replicated
- gain_grad: float32 [2, 1024], replicated
- shift_grad: float32 [2, 1024], replicated
Inputs may be any that keep to these rules, and one draw needn't show every extreme that they name: `segment_ids`: in each sequence documents are numbered 0 to 7 in order, each 1 to 1280 tokens long, one exactly 1280.
All inputs are finite; a program needn't handle non-finite values.
Results may differ from a plain program's by a relative error of at most 0.018.
Values may be sent and summed in bfloat16 or wider, within the bound.
A program may use at most 192 MiB of HBM per device.

v0:
```python
import math
import jax
import jax.numpy as jnp
from jax import lax
from jax.sharding import PartitionSpec as P

HEADS = 16
NEGATIVE = -1e30


def normalize(hidden, gain, shift):
    center = hidden - jnp.mean(hidden, axis=-1, keepdims=True)
    spread = jnp.mean(center * center, axis=-1, keepdims=True)
    return center * lax.rsqrt(spread + 1e-05) * gain + shift


def exact_gelu(value):
    return jax.nn.gelu(value, approximate=False)


def gather_attention(qkv_weight, out_weight):
    return (
        lax.all_gather(qkv_weight, "fsdp", axis=0, tiled=True),
        lax.all_gather(out_weight, "fsdp", axis=0, tiled=True),
    )


def gather_feedforward(up_weight, down_weight):
    return (
        lax.all_gather(up_weight, "fsdp", axis=0, tiled=True),
        lax.all_gather(down_weight, "fsdp", axis=0, tiled=True),
    )


def block_plan(row_count):
    block_rows = math.gcd(row_count, 1024)
    return (block_rows, row_count // block_rows)


def split_heads(matrix):
    return matrix.reshape(matrix.shape[0], HEADS, matrix.shape[1] // HEADS)


def join_heads(stacked):
    return jnp.transpose(stacked, (1, 0, 2)).reshape(
        stacked.shape[1], stacked.shape[0] * stacked.shape[2]
    )


def local(
    tokens,
    segment_ids,
    qkv_weight,
    out_weight,
    up_weight,
    down_weight,
    proj_bias,
    hidden_bias,
    norm_gain,
    norm_shift,
    cotangent,
):
    inputs = tokens[0]
    tok_count, model_width = inputs.shape
    head_dim = model_width // HEADS
    score_scale = head_dim ** (-0.5)
    doc_ids = segment_ids[0]
    own_index = lax.axis_index("fsdp")
    own_docs = lax.dynamic_slice_in_dim(doc_ids, own_index * tok_count, tok_count)
    qkv_full, out_full = gather_attention(qkv_weight, out_weight)
    projected = jnp.dot(inputs, qkv_full, preferred_element_type=jnp.float32)
    queries = (projected[:, :model_width] + proj_bias[0]).astype(jnp.bfloat16)
    key_rows = projected[:, model_width : 2 * model_width].astype(jnp.bfloat16)
    value_rows = (projected[:, 2 * model_width :] + proj_bias[1]).astype(jnp.bfloat16)
    query_heads = split_heads(queries)
    key_own = split_heads(key_rows)
    value_own = split_heads(value_rows)
    initial = (
        jnp.zeros((HEADS, tok_count, head_dim), jnp.float32),
        jnp.full((HEADS, tok_count), NEGATIVE, jnp.float32),
        jnp.zeros((HEADS, tok_count), jnp.float32),
    )
    key_piece = lax.all_gather(key_rows, "fsdp", axis=0, tiled=True)
    value_piece = lax.all_gather(value_rows, "fsdp", axis=0, tiled=True)
    block_rows, blocks = block_plan(key_piece.shape[0])

    def forward_advance(block_index, running_state):
        weighted, running, denominator = running_state
        offset = block_index * block_rows
        key_block = split_heads(lax.dynamic_slice_in_dim(key_piece, offset, block_rows))
        value_block = split_heads(lax.dynamic_slice_in_dim(value_piece, offset, block_rows))
        block_docs = lax.dynamic_slice_in_dim(doc_ids, offset, block_rows)
        scores = (
            jnp.einsum("qhd,khd->hqk", query_heads, key_block, preferred_element_type=jnp.float32)
            * score_scale
        )
        same_doc = (own_docs[:, None] == block_docs[None, :])[None]
        highest = jnp.maximum(running, jnp.max(jnp.where(same_doc, scores, NEGATIVE), axis=2))
        factor = jnp.exp(running - highest)
        weights = jnp.where(same_doc, jnp.exp(scores - highest[:, :, None]), 0.0)
        denominator = denominator * factor + jnp.sum(weights, axis=2)
        weighted = weighted * factor[:, :, None] + jnp.einsum(
            "hqk,khd->hqd",
            weights.astype(jnp.bfloat16),
            value_block,
            preferred_element_type=jnp.float32,
        )
        return (weighted, highest, denominator)

    weighted, running, denominator = lax.fori_loop(0, blocks, forward_advance, initial)
    attended_heads = weighted / denominator[:, :, None]
    log_total = running + jnp.log(denominator)
    attended_low = join_heads(attended_heads).astype(jnp.bfloat16)
    branch = jnp.dot(attended_low, out_full, preferred_element_type=jnp.float32) + proj_bias[2]
    first_norm, norm_one_back = jax.vjp(
        normalize, inputs.astype(jnp.float32) + branch, norm_gain[0], norm_shift[0]
    )
    first_low = first_norm.astype(jnp.bfloat16)
    up_full, down_full = gather_feedforward(up_weight, down_weight)
    hidden_pre = jnp.dot(first_low, up_full, preferred_element_type=jnp.float32) + hidden_bias
    activated, gelu_back = jax.vjp(exact_gelu, hidden_pre)
    activated_low = activated.astype(jnp.bfloat16)
    second = jnp.dot(activated_low, down_full, preferred_element_type=jnp.float32) + proj_bias[3]
    output, norm_two_back = jax.vjp(normalize, first_norm + second, norm_gain[1], norm_shift[1])
    up_back, down_back = gather_feedforward(up_weight, down_weight)
    qkv_back, out_back = gather_attention(qkv_weight, out_weight)
    grad_second, gain_two, shift_two = norm_two_back(cotangent[0].astype(jnp.float32))
    second_low = grad_second.astype(jnp.bfloat16)
    down_term = jnp.einsum(
        "tf,td->fd", activated_low, second_low, preferred_element_type=jnp.float32
    )
    activated_grad = jnp.einsum(
        "td,fd->tf", second_low, down_back, preferred_element_type=jnp.float32
    )
    (pre_grad,) = gelu_back(activated_grad)
    pre_low = pre_grad.astype(jnp.bfloat16)
    up_term = jnp.einsum("td,tf->df", first_low, pre_low, preferred_element_type=jnp.float32)
    first_grad = grad_second + jnp.einsum(
        "tf,df->td", pre_low, up_back, preferred_element_type=jnp.float32
    )
    branch_grad, gain_one, shift_one = norm_one_back(first_grad)
    branch_low = branch_grad.astype(jnp.bfloat16)
    out_term = jnp.einsum("te,td->ed", attended_low, branch_low, preferred_element_type=jnp.float32)
    attended_grad = jnp.einsum(
        "td,ed->te", branch_low, out_back, preferred_element_type=jnp.float32
    ).astype(jnp.bfloat16)
    grad_heads = split_heads(attended_grad)
    correction = jnp.einsum("qhd,hqd->hq", grad_heads.astype(jnp.float32), attended_heads)
    lse_all, correction_all = (
        lax.all_gather(log_total, "fsdp", axis=1, tiled=True),
        lax.all_gather(correction, "fsdp", axis=1, tiled=True),
    )
    query_key_piece = lax.all_gather(key_rows, "fsdp", axis=0, tiled=True)
    query_value_piece = lax.all_gather(value_rows, "fsdp", axis=0, tiled=True)
    query_block_rows, blocks = block_plan(query_key_piece.shape[0])

    def query_advance(block_index, query_state):
        offset = block_index * query_block_rows
        key_block = split_heads(lax.dynamic_slice_in_dim(query_key_piece, offset, query_block_rows))
        value_block = split_heads(
            lax.dynamic_slice_in_dim(query_value_piece, offset, query_block_rows)
        )
        block_docs = lax.dynamic_slice_in_dim(doc_ids, offset, query_block_rows)
        scores = (
            jnp.einsum("qhd,khd->hqk", query_heads, key_block, preferred_element_type=jnp.float32)
            * score_scale
        )
        same_doc = (own_docs[:, None] == block_docs[None, :])[None]
        probabilities = jnp.where(same_doc, jnp.exp(scores - log_total[:, :, None]), 0.0)
        prob_grad = jnp.einsum(
            "qhd,khd->hqk", grad_heads, value_block, preferred_element_type=jnp.float32
        )
        score_grad = (probabilities * (prob_grad - correction[:, :, None])).astype(jnp.bfloat16)
        return query_state + jnp.einsum(
            "hqk,khd->hqd", score_grad, key_block, preferred_element_type=jnp.float32
        )

    query_acc = lax.fori_loop(
        0, blocks, query_advance, jnp.zeros((HEADS, tok_count, head_dim), jnp.float32)
    )
    query_grad = (join_heads(query_acc) * score_scale).astype(jnp.bfloat16)
    empty_heads = jnp.zeros((HEADS, tok_count, head_dim), jnp.float32)
    query_piece = lax.all_gather(queries, "fsdp", axis=0, tiled=True)
    grad_piece = lax.all_gather(attended_grad, "fsdp", axis=0, tiled=True)
    key_block_rows, blocks = block_plan(query_piece.shape[0])

    def key_advance(block_index, key_state):
        key_acc, value_acc = key_state
        offset = block_index * key_block_rows
        query_block = split_heads(lax.dynamic_slice_in_dim(query_piece, offset, key_block_rows))
        grad_block = split_heads(lax.dynamic_slice_in_dim(grad_piece, offset, key_block_rows))
        block_docs = lax.dynamic_slice_in_dim(doc_ids, offset, key_block_rows)
        lse_block = lax.dynamic_slice_in_dim(lse_all, offset, key_block_rows, axis=1)
        corr_block = lax.dynamic_slice_in_dim(correction_all, offset, key_block_rows, axis=1)
        scores = (
            jnp.einsum("qhd,khd->hqk", query_block, key_own, preferred_element_type=jnp.float32)
            * score_scale
        )
        same_doc = (block_docs[:, None] == own_docs[None, :])[None]
        probabilities = jnp.where(same_doc, jnp.exp(scores - lse_block[:, :, None]), 0.0)
        value_acc = value_acc + jnp.einsum(
            "hqk,qhd->hkd",
            probabilities.astype(jnp.bfloat16),
            grad_block,
            preferred_element_type=jnp.float32,
        )
        prob_grad = jnp.einsum(
            "qhd,khd->hqk", grad_block, value_own, preferred_element_type=jnp.float32
        )
        score_grad = (probabilities * (prob_grad - corr_block[:, :, None])).astype(jnp.bfloat16)
        key_acc = key_acc + jnp.einsum(
            "hqk,qhd->hkd", score_grad, query_block, preferred_element_type=jnp.float32
        )
        return (key_acc, value_acc)

    key_acc, value_acc = lax.fori_loop(0, blocks, key_advance, (empty_heads, empty_heads))
    key_grad = (join_heads(key_acc) * score_scale).astype(jnp.bfloat16)
    value_grad = join_heads(value_acc).astype(jnp.bfloat16)
    qkv_grad_low = jnp.concatenate([query_grad, key_grad, value_grad], axis=1)
    qkv_term = jnp.einsum("td,te->de", inputs, qkv_grad_low, preferred_element_type=jnp.float32)
    input_grad = branch_grad + jnp.einsum(
        "te,de->td", qkv_grad_low, qkv_back, preferred_element_type=jnp.float32
    )
    bias_term = jnp.stack(
        [
            jnp.sum(query_grad.astype(jnp.float32), axis=0),
            jnp.sum(value_grad.astype(jnp.float32), axis=0),
            jnp.sum(branch_low.astype(jnp.float32), axis=0),
            jnp.sum(second_low.astype(jnp.float32), axis=0),
        ]
    )
    hidden_term = jnp.sum(pre_low.astype(jnp.float32), axis=0)
    gain_term = jnp.stack([gain_one, gain_two])
    shift_term = jnp.stack([shift_one, shift_two])
    bias_total, hidden_total, gain_total, shift_total = lax.psum(
        (bias_term, hidden_term, gain_term, shift_term), ("rep", "fsdp")
    )
    up_sum, down_sum = (
        lax.psum_scatter(up_term, "fsdp", scatter_dimension=0, tiled=True),
        lax.psum_scatter(down_term, "fsdp", scatter_dimension=0, tiled=True),
    )
    qkv_sum, out_sum = (
        lax.psum_scatter(qkv_term, "fsdp", scatter_dimension=0, tiled=True),
        lax.psum_scatter(out_term, "fsdp", scatter_dimension=0, tiled=True),
    )
    qkv_total, out_total, up_total, down_total = lax.psum(
        (qkv_sum, out_sum, up_sum, down_sum), "rep"
    )
    grad_scale = (tok_count * lax.axis_size("fsdp") * lax.axis_size("rep")) ** (-0.5)
    return (
        output.astype(jnp.bfloat16)[None],
        input_grad.astype(jnp.bfloat16)[None],
        qkv_total * grad_scale,
        out_total * grad_scale,
        up_total * grad_scale,
        down_total * grad_scale,
        bias_total * grad_scale,
        hidden_total * grad_scale,
        gain_total * grad_scale,
        shift_total * grad_scale,
    )


def solution(mesh):
    return jax.shard_map(
        local,
        mesh=mesh,
        in_specs=(
            P("rep", "fsdp", None),
            P("rep", None),
            P("fsdp", None),
            P("fsdp", None),
            P("fsdp", None),
            P("fsdp", None),
            P(),
            P(),
            P(),
            P(),
            P("rep", "fsdp", None),
        ),
        out_specs=(
            P("rep", "fsdp", None),
            P("rep", "fsdp", None),
            P("fsdp", None),
            P("fsdp", None),
            P("fsdp", None),
            P("fsdp", None),
            P(),
            P(),
            P(),
            P(),
        ),
        check_vma=False,
    )
```

profile of v0, /device:TPU:0, one launch (start us, length us, event | category | flops | bytes accessed | tf_op | source)
XLA Modules:
  0.0 996.0 jit_solution(13008734010927375678)
XLA Ops:
  8.8 49.3 %all-gather.9.cloned.1.call-done = bf16[1024,3072]{1,0:T(8,128)(2,1)} async-done(((bf16[128,3072]{1,0:T(8,128)(2,1)}), bf16[1024,3072]{1,0:T(8,128)(2,1)}) %all-gather.9.cloned.1.call-update) | async-done | bytes 6291472 | tf_op jit(solution)/shard_map/all_gather | solution.py:23
  58.2 4.8 fusion.60
  70.8 31.7 %all-gather.13.cloned.1.call-done = bf16[2048,1024]{1,0:T(8,128)(2,1)} async-done(((bf16[256,1024]{1,0:T(8,128)(2,1)}), bf16[2048,1024]{1,0:T(8,128)(2,1)}) %all-gather.13.cloned.1.call-update) | async-done | bytes 4194320 | tf_op jit(solution)/shard_map/all_gather | solution.py:84
  102.5 6.4 copy.33
  109.0 32.8 %all-gather.11.cloned.1.call-done = bf16[2048,1024]{1,0:T(8,128)(2,1)} async-done(((bf16[256,1024]{1,0:T(8,128)(2,1)}), bf16[2048,1024]{1,0:T(8,128)(2,1)}) %all-gather.11.cloned.1.call-update) | async-done | bytes 4194320 | tf_op jit(solution)/shard_map/all_gather | solution.py:83
  141.8 6.5 copy.32
  148.2 59.9 %while.48 = (s32[]{:T(128)}, f32[16,256,64]{1,2,0:T(8,128)}, f32[16,256]{1,0:T(8,128)S(1)}, f32[16,256]{1,0:T(8,128)S(1)}, s32[256]{0:T(256)S(1)}, /*index=5*/s3...) while((s32[]{:T(128)}, f32[16,256,64]{1,2,0:T(8,128)}, ...), condition=%wide.region_3.4_spmd.clone, body=%wide.region_0.3_spmd.clone.sunk | while | flops 1120948224 | bytes 75248888 | solution.py:110
  152.0 7.3 fusion.139
  159.3 9.5 fusion.140
  168.9 7.7 fusion.142
  181.6 7.3 fusion.139
  188.9 9.2 fusion.140
  198.1 9.0 fusion.142
  212.4 15.2 %all-gather.17.cloned.1.call-done = bf16[1024,4096]{1,0:T(8,128)(2,1)} async-done(((bf16[128,4096]{1,0:T(8,128)(2,1)}), bf16[1024,4096]{1,0:T(8,128)(2,1)}) %all-gather.17.cloned.1.call-update) | async-done | bytes 8388624 | tf_op jit(solution)/shard_map/all_gather | solution.py:30
  227.6 16.2 %multiply_convert_fusion.1 = (bf16[256,4096]{1,0:T(8,128)(2,1)}, f32[256,4096]{1,0:T(8,128)}, f32[256,4096]{1,0:T(8,128)}) fusion(f32[4096]{0:T(1024)S(1)} %copy-done.39, bf16[1024,4096]{1,0:T(8,128)(2,1)} %all-gather.17.cloned.1.call-done, f32[256,1024]{1,0:T(8,128)S(1)} %get-tuple-element.818, f32[1024]{0:T(1024)S(1)} %bitcast.204, ...), kind=kOutput, calls=%fused_computation.57 | convolution fusion | flops 2218000384 | bytes 19949568 | tf_op jit(solution)/shard_map/dot_general | solution.py:120
  243.8 39.9 %all-gather.19.cloned.1.call-done = bf16[4096,1024]{1,0:T(8,128)(2,1)} async-done(((bf16[512,1024]{1,0:T(8,128)(2,1)}), bf16[4096,1024]{1,0:T(8,128)(2,1)}) %all-gather.19.cloned.1.call-update) | async-done | bytes 8388624 | tf_op jit(solution)/shard_map/all_gather | solution.py:31
  283.8 6.5 fusion.77
  293.7 12.6 %convert_reduce_fusion = (f32[4096]{0:T(1024)}, bf16[256,4096]{1,0:T(8,128)(2,1)S(1)}) fusion(f32[256,4096]{1,0:T(8,128)} %get-tuple-element.795, f32[256,4096]{1,0:T(8,128)} %get-tuple-element.819, bf16[256,1024]{1,0:T(8,128)(2,1)S(1)} %get-tuple-element.789, bf16[4096,1024]{1,0:T(8,128)(2,1)} %all-gather.19.cloned.1.call-done), kind=kOutput, calls=%fused_computation.55 | convolution fusion | flops 2164256768 | bytes 19415040 | tf_op jit(solution)/shard_map/td,fd->tf/dot_general | solution.py:132
  316.3 9.9 fusion.67
  327.7 8.4 fusion.80
  345.1 9.6 all_gather.45
  356.1 10.0 %all_gather.43 = f32[16,2048]{1,0:T(8,128)} all-gather(f32[16,256]{1,0:T(8,128)} %log_add_fusion), channel_id=1, replica_groups=mesh['rep'=4,'fsdp'=8] {'fsdp'}, dimensions={1}, use_global_device_ids=true | all-gather | bytes 147456 | tf_op jit(solution)/shard_map/all_gather | solution.py:150
  366.1 53.6 %while.49 = (s32[]{:T(128)}, f32[16,256,64]{1,2,0:T(8,128)}, s32[256]{0:T(256)}, s32[2048]{0:T(1024)}, bf16[2048,1024]{0,1:T(8,128)(2,1)}, /*index=5*/bf16[256,1...) while((s32[]{:T(128)}, f32[16,256,64]{1,2,0:T(8,128)}, ...), condition=%wide.region_13.14_spmd.clone, body=%wide.region_12.13_spmd.clone.sunk | while | flops 1636564992 | bytes 51954912 | solution.py:178
  366.1 4.0 constant_dynamic-slice_fusion.14
  370.1 9.4 fusion.148
  380.4 13.0 %fusion.149 = f32[16,256,64]{1,2,0:T(8,128)} fusion(bf16[1024,16,64]{0,2,1:T(8,128)(2,1)S(1)} %bitcast.178, f32[16,1024,256]{1,2,0:T(8,128)} %fusion.148, bf16[1024,16,64]{0,2,1:T(8,128)(2,1)} %bitcast.185, f32[16,256]{1,0:T(8,128)} %get-tuple-element.1154, f32[16,256]{1,0:T(8,128)} %get-tuple-element.1151, ...), kind=kOutput, calls=%fused_computation.24.clone.1 | convolution fusion | flops 1099431936 | bytes 23887872 | tf_op jit(solution)/shard_map/while/body/eval_jaxpr/hqk,khd->hqd/dot_general | solution.py:174
  393.4 4.0 constant_dynamic-slice_fusion.14
  397.4 8.1 fusion.148
  406.3 13.3 %fusion.149 = f32[16,256,64]{1,2,0:T(8,128)} fusion(bf16[1024,16,64]{0,2,1:T(8,128)(2,1)S(1)} %bitcast.178, f32[16,1024,256]{1,2,0:T(8,128)} %fusion.148, bf16[1024,16,64]{0,2,1:T(8,128)(2,1)} %bitcast.185, f32[16,256]{1,0:T(8,128)} %get-tuple-element.1154, f32[16,256]{1,0:T(8,128)} %get-tuple-element.1151, ...), kind=kOutput, calls=%fused_computation.24.clone.1 | convolution fusion | flops 1099431936 | bytes 23887872 | tf_op jit(solution)/shard_map/while/body/eval_jaxpr/hqk,khd->hqd/dot_general | solution.py:174
  421.8 90.0 %while.50 = (s32[]{:T(128)}, f32[16,256,64]{1,2,0:T(8,128)}, f32[16,256,64]{1,2,0:T(8,128)}, s32[2048]{0:T(1024)}, s32[256]{0:T(256)}, /*index=5*/bf16[2048,1024...) while((s32[]{:T(128)}, f32[16,256,64]{1,2,0:T(8,128)}, ...), condition=%wide.region_15.16_spmd.clone, body=%wide.region_14.15_spmd.clone.sunk | while | flops 2190737408 | bytes 84624672 | solution.py:216
  422.0 4.7 constant_dynamic-slice_fusion.15
  429.7 11.4 %fusion.157 = f32[16,1024,256]{2,1,0:T(8,128)} fusion(bf16[1024,16,64]{0,2,1:T(8,128)(2,1)S(1)} %bitcast.179, bf16[256,16,64]{0,2,1:T(8,128)(2,1)S(1)} %copy-done.2), kind=kOutput, calls=%fused_computation.152.clone.1 | convolution fusion | flops 536870912 | bytes 19398656 | tf_op jit(solution)/shard_map/while/body/eval_jaxpr/qhd,khd->hqk/dot_general | solution.py:196
  441.1 4.2 copy.76
  446.3 9.3 fusion.159
  455.6 12.7 %fusion.158 = f32[16,256,64]{1,2,0:T(8,128)} fusion(bf16[1024,16,64]{0,2,1:T(8,128)(2,1)S(1)} %bitcast.180, f32[16,1024,256]{2,1,0:T(8,128)} %fusion.157, bf16[1024,16,64]{0,2,1:T(8,128)(2,1)} %bitcast.183, f32[16,1024]{1,0:T(8,128)S(1)} %get-tuple-element.1031, f32[16,1024]{1,0:T(8,128)S(1)} %get-tuple-element.1032, ...), kind=kOutput, calls=%fused_computation.40.clone.1 | convolution fusion | flops 1099431936 | bytes 23986176 | tf_op jit(solution)/shard_map/while/body/eval_jaxpr/hqk,qhd->hkd/dot_general | solution.py:211
  468.3 4.7 constant_dynamic-slice_fusion.15
  476.0 8.5 fusion.157
  484.5 4.1 copy.76
  489.5 9.9 fusion.159
  499.5 12.3 %fusion.158 = f32[16,256,64]{1,2,0:T(8,128)} fusion(bf16[1024,16,64]{0,2,1:T(8,128)(2,1)S(1)} %bitcast.180, f32[16,1024,256]{2,1,0:T(8,128)} %fusion.157, bf16[1024,16,64]{0,2,1:T(8,128)(2,1)} %bitcast.183, f32[16,1024]{1,0:T(8,128)S(1)} %get-tuple-element.1031, f32[16,1024]{1,0:T(8,128)S(1)} %get-tuple-element.1032, ...), kind=kOutput, calls=%fused_computation.40.clone.1 | convolution fusion | flops 1099431936 | bytes 23986176 | tf_op jit(solution)/shard_map/while/body/eval_jaxpr/hqk,qhd->hkd/dot_general | solution.py:211
  514.4 7.4 convolution_bitcast_fusion
  521.9 14.2 %reduce-scatter.9.cloned.1.call-done = f32[128,4096]{1,0:T(8,128)} async-done(((f32[1024,4096]{1,0:T(8,128)}), f32[128,4096]{1,0:T(8,128)}) %reduce-scatter.9.cloned.1.call-update) | async-done | bytes 2097168 | tf_op jit(solution)/shard_map/reduce_scatter | solution.py:239
  536.2 120.0 %reduce-scatter.11.cloned.1.call-done = f32[512,1024]{1,0:T(8,128)} async-done(((f32[4096,1024]{1,0:T(8,128)}), f32[512,1024]{1,0:T(8,128)}) %reduce-scatter.11.cloned.1.call-update) | async-done | bytes 2097168 | tf_op jit(solution)/shard_map/reduce_scatter | solution.py:240
  656.1 96.2 %reduce-scatter.5.cloned.1.call-done = f32[128,3072]{0,1:T(8,128)} async-done(((f32[1024,3072]{0,1:T(8,128)}), f32[128,3072]{0,1:T(8,128)}) %reduce-scatter.5.cloned.1.call-update) | async-done | bytes 1572880 | tf_op jit(solution)/shard_map/reduce_scatter | solution.py:243
  752.7 48.6 %all-reduce = (f32[4,1024]{1,0:T(4,128)S(1)}, f32[4096]{0:T(1024)S(1)}, f32[2,1024]{1,0:T(2,128)S(1)}, f32[2,1024]{1,0:T(2,128)S(1)}) all-reduce(f32[4,1024]{1,0:T(4,128)S(1)} %pad_maximum_fusion.3, f32[4096]{0:T(1024)S(1)} %copy-done.32, f32[2,1024]{1,0:T(2,128)S(1)} %get-tuple-element.824, ...), channel_id=1, replica_groups=mesh['rep'=4,'fsdp'=8] {'rep','fsdp'}, use_global_device_ids=true, to_apply=%region_28.29 | all-reduce | flops 12288 | bytes 98304 | tf_op jit(solution)/shard_map/psum | solution.py:235
  803.7 5.6 fusion.51
  809.2 170.8 %all-reduce.4.cloned.1.call-done = (f32[128,3072]{0,1:T(8,128)}, f32[128,1024]{1,0:T(8,128)}, f32[128,4096]{1,0:T(8,128)}, f32[512,1024]{1,0:T(8,128)}) async-done(((f32[128,3072]{0,1:T(8,128)}, f32[128,1024]{1,0:T(8,128)}, f32[128,4096]{1,0:T(8,128)}, f32[512,1024]{1,0:T(8,128)}), (f32[128,3072]{0,1:T(8,128)}, f32[128,1024]{1,0:T(8,128)}, f32[128,4096]{1,0:T(8,128)}, ...) | async-done | bytes 6291472 | tf_op jit(solution)/shard_map/psum | solution.py:246
  983.2 3.4 broadcast_multiply_fusion
  (207 shorter events, 71.2 us)
Async XLA Ops:
  7.2 51.0 %all-gather.9.cloned.1.call-start = ((), (), s32[]{:S(2)}) async-start(), calls=%async_computation.4 | async-start | bytes 7077888 | tf_op jit(solution)/shard_map/all_gather | solution.py:23
  7.9 94.6 %all-gather.13.cloned.1.call-start = ((), (), s32[]{:S(2)}) async-start(), calls=%async_computation.6 | async-start | bytes 4718592 | tf_op jit(solution)/shard_map/all_gather | solution.py:84
  62.9 7.6 copy-start.33
  62.9 7.6 copy-start.34
  65.6 5.1 copy-start.6
  65.7 76.1 %all-gather.11.cloned.1.call-start = ((), (), s32[]{:S(2)}) async-start(), calls=%async_computation.5 | async-start | bytes 4718592 | tf_op jit(solution)/shard_map/all_gather | solution.py:83
  68.0 141.7 %all-gather.15.cloned.1.call-start = ((), (), s32[]{:S(2)}) async-start(), calls=%async_computation.7 | async-start | bytes 2359296 | tf_op jit(solution)/shard_map/all_gather | solution.py:24
  68.5 159.0 %all-gather.17.cloned.1.call-start = ((), (), s32[]{:S(2)}) async-start(), calls=%async_computation.8 | async-start | bytes 9437184 | tf_op jit(solution)/shard_map/all_gather | solution.py:30
  69.1 214.6 %all-gather.19.cloned.1.call-start = ((), (), s32[]{:S(2)}) async-start(), calls=%async_computation.9 | async-start | bytes 9437184 | tf_op jit(solution)/shard_map/all_gather | solution.py:31
  69.7 352.1 %all-gather.21.cloned.1.call-start = ((), (), s32[]{:S(2)}) async-start(), calls=%async_computation.10 | async-start | bytes 4718592 | tf_op jit(solution)/shard_map/all_gather | solution.py:183
  70.8 351.0 %all-gather.23.cloned.1.call-start = ((), (), s32[]{:S(2)}) async-start(), calls=%async_computation.11 | async-start | bytes 4718592 | tf_op jit(solution)/shard_map/all_gather | solution.py:184
  148.2 61.5 %copy-start.15 = (bf16[1,256,1024]{2,1,0:T(8,128)(2,1)S(1)}, bf16[1,256,1024]{2,1,0:T(8,128)(2,1)}, u32[]{:S(2)}) copy-start(bf16[1,256,1024]{2,1,0:T(8,128)(2,1)} %param.17) | copy-start | bytes 1572868
  159.3 9.6 copy-start.10
  188.9 9.2 copy-start.10
  208.1 35.7 %copy-start = (bf16[256,16,64]{0,2,1:T(8,128)(2,1)}, bf16[256,16,64]{0,2,1:T(8,128)(2,1)S(1)}, u32[]{:S(2)}) copy-start(bf16[256,16,64]{0,2,1:T(8,128)(2,1)S(1)} %get-tuple-element.1191) | copy-start | bytes 1572868
  208.1 35.7 %copy-start.26 = (s32[256]{0:T(256)}, s32[256]{0:T(256)S(1)}, u32[]{:S(2)}) copy-start(s32[256]{0:T(256)S(1)} %get-tuple-element.1223) | copy-start | bytes 3076
  208.1 136.2 %copy-start.24 = (f32[16,256]{1,0:T(8,128)}, f32[16,256]{1,0:T(8,128)S(1)}, u32[]{:S(2)}) copy-start(f32[16,256]{1,0:T(8,128)S(1)} %get-tuple-element.521) | copy-start | bytes 49156
  208.1 19.5 %copy-start.39 = (f32[4096]{0:T(1024)S(1)}, f32[4096]{0:T(1024)}, u32[]{:S(2)}) copy-start(f32[4096]{0:T(1024)} %param.24) | copy-start | bytes 49156
  283.8 6.8 copy-start.4
  291.6 14.7 %slice-start = ((s8[8388608]{0:T(1024)(128)(4,1)}), s8[4194304]{0:T(1024)(128)(4,1)S(1)}, s32[]{:S(2)}) async-start(s8[8388608]{0:T(1024)(128)(4,1)} %bitcast.220), calls=%async_computation.17 | async-start | bytes 8388608
  293.7 12.6 %slice-start.1 = ((s8[8388608]{0:T(1024)(128)(4,1)}), s8[4194304]{0:T(1024)(128)(4,1)S(1)}, s32[]{:S(2)}) async-start(s8[8388608]{0:T(1024)(128)(4,1)} %bitcast.220), calls=%async_computation.18 | async-start | bytes 8388608
  310.0 6.2 copy-start.37
  313.4 208.6 %reduce-scatter.7.cloned.1.call-start = ((), (), s32[]{:S(2)}) async-start(), calls=%async_computation.13 | async-start | bytes 4718592 | tf_op jit(solution)/shard_map/reduce_scatter | solution.py:244
  316.2 219.9 %reduce-scatter.9.cloned.1.call-start = ((), (), s32[]{:S(2)}) async-start(), calls=%async_computation.14 | async-start | bytes 18874368 | tf_op jit(solution)/shard_map/reduce_scatter | solution.py:239
  326.1 330.0 %reduce-scatter.11.cloned.1.call-start = ((), (), s32[]{:S(2)}) async-start(), calls=%async_computation.15 | async-start | bytes 18874368 | tf_op jit(solution)/shard_map/reduce_scatter | solution.py:240
  336.1 416.2 %reduce-scatter.5.cloned.1.call-start = ((), (), s32[]{:S(2)}) async-start(), calls=%async_computation.12 | async-start | bytes 14155776 | tf_op jit(solution)/shard_map/reduce_scatter | solution.py:243
  338.3 6.0 copy-start.12
  370.1 10.1 %copy-start.27 = (s32[256]{0:T(256)S(1)}, s32[256]{0:T(256)}, u32[]{:S(2)}) copy-start(s32[256]{0:T(256)} %get-tuple-element.1147) | copy-start | bytes 3076 | tf_op jit(solution)/shard_map/while
  397.4 8.7 copy-start.27
  421.8 92.6 %copy-start.16 = (bf16[1,256,1024]{2,1,0:T(8,128)(2,1)S(1)}, bf16[1,256,1024]{2,1,0:T(8,128)(2,1)}, u32[]{:S(2)}) copy-start(bf16[1,256,1024]{2,1,0:T(8,128)(2,1)} %param.17) | copy-start | bytes 1572868
  441.1 4.2 copy-start.23
  441.1 5.0 copy-start.28
  484.5 4.1 copy-start.23
  484.5 4.8 copy-start.28
  521.8 230.6 %copy-start.5 = (bf16[1,256,1024]{2,1,0:T(8,128)(2,1)S(1)}, bf16[1,256,1024]{2,1,0:T(8,128)(2,1)}, u32[]{:S(2)}) copy-start(bf16[1,256,1024]{2,1,0:T(8,128)(2,1)} %param.27) | copy-start | bytes 1572868
  521.8 230.8 %copy-start.29 = (f32[1024]{0:T(1024)S(1)}, f32[1024]{0:T(1024)}, u32[]{:S(2)}) copy-start(f32[1024]{0:T(1024)} %get-tuple-element.707) | copy-start | bytes 12292
  521.8 230.7 %copy-start.35 = (f32[1024]{0:T(1024)S(1)}, f32[1024]{0:T(1024)}, u32[]{:S(2)}) copy-start(f32[1024]{0:T(1024)} %get-tuple-element.705) | copy-start | bytes 12292
  521.8 230.7 %copy-start.36 = (f32[1024]{0:T(1024)S(1)}, f32[1024]{0:T(1024)}, u32[]{:S(2)}) copy-start(f32[1024]{0:T(1024)} %get-tuple-element.709) | copy-start | bytes 12292
  521.8 230.8 %copy-start.30 = (f32[1024]{0:T(1024)S(1)}, f32[1024]{0:T(1024)}, u32[]{:S(2)}) copy-start(f32[1024]{0:T(1024)} %get-tuple-element.788) | copy-start | bytes 12292
  521.8 230.8 %copy-start.31 = (f32[1024]{0:T(1024)S(1)}, f32[1024]{0:T(1024)}, u32[]{:S(2)}) copy-start(f32[1024]{0:T(1024)} %get-tuple-element.786) | copy-start | bytes 12292
  521.8 230.8 %copy-start.32 = (f32[4096]{0:T(1024)S(1)}, f32[4096]{0:T(1024)}, u32[]{:S(2)}) copy-start(f32[4096]{0:T(1024)} %get-tuple-element.780) | copy-start | bytes 49156
  521.8 281.8 %copy-start.9 = (f32[256,1024]{1,0:T(8,128)S(1)}, f32[256,1024]{1,0:T(8,128)}, u32[]{:S(2)}) copy-start(f32[256,1024]{1,0:T(8,128)} %copy-done.8) | copy-start | bytes 3145732
  521.8 281.8 %copy-start.17 = (bf16[16,256,64]{1,2,0:T(8,128)(2,1)S(1)}, bf16[16,256,64]{1,2,0:T(8,128)(2,1)}, u32[]{:S(2)}) copy-start(bf16[16,256,64]{1,2,0:T(8,128)(2,1)} %get-tuple-element.783) | copy-start | bytes 1572868
  521.9 281.8 %copy-start.21 = (bf16[16,256,64]{1,2,0:T(8,128)(2,1)S(1)}, bf16[16,256,64]{1,2,0:T(8,128)(2,1)}, u32[]{:S(2)}) copy-start(bf16[16,256,64]{1,2,0:T(8,128)(2,1)} %copy-done.20) | copy-start | bytes 1572868
  521.9 281.8 %copy-start.38 = (f32[256]{0:T(256)S(1)}, f32[256]{0:T(256)}, u32[]{:S(2)}) copy-start(f32[256]{0:T(256)} %copy-done.37) | copy-start | bytes 3076
  521.9 458.2 %all-reduce.4.cloned.1.call-start = ((), (), s32[]{:S(2)}) async-start(), calls=%async_computation.16 | async-start | bytes 12582912 | tf_op jit(solution)/shard_map/psum | solution.py:246
  983.2 3.4 copy-start.19
  983.2 5.0 copy-start.25
  (13 other events, 23.7 us)
Sparse Core Ops, SparseCore 0:
  9.9 48.2 all-gather.8
  65.8 36.7 all-gather.12
  105.0 36.7 all-gather.10
  143.5 27.8 all-gather.14
  173.2 54.3 all-gather.16
  229.3 54.3 all-gather.18
  285.6 36.7 all-gather.20
  324.3 37.2 all-gather.22
  364.9 51.3 reduce-scatter.6
  420.2 115.9 reduce-scatter.8
  540.1 115.9 reduce-scatter.10
  659.9 92.3 reduce-scatter.4
  755.1 224.8 all-reduce.3
where the time goes:
time: 1010 us; the launch traced here: 996 us
  waiting for transfers between devices  573 us (57%)
  matrix products  220 us (22%)
  local copies, waits for them, and re-layouts  75.5 us (7%)
  blocking collectives  68.2 us (7%)
  other arithmetic  43.3 us (4%)
  between operations  14.8 us (1%)
    psum x1, waiting for transfers between devices, local(): lax.psum((qkv_sum, out_sum, up_sum, down_sum), 'rep')  171 us
    reduce_scatter x1, waiting for transfers between devices, local(): lax.psum_scatter(down_term, 'fsdp', scatter_dimension=0, tiled=True)  120 us
    reduce_scatter x1, waiting for transfers between devices, local(): lax.psum_scatter(qkv_term, 'fsdp', scatter_dimension=0, tiled=True)  96.2 us
    all_gather x1, waiting for transfers between devices, gather_attention(): lax.all_gather(qkv_weight, 'fsdp', axis=0, tiled=True)  49.3 us
    psum x1, blocking collectives, local(): lax.psum((bias_term, hidden_term, gain_term, shift_term), ('rep', 'fsdp'))  48.6 us
    all_gather x1, waiting for transfers between devices, gather_feedforward(): lax.all_gather(down_weight, 'fsdp', axis=0, tiled=True)  39.9 us
    all_gather x1, waiting for transfers between devices, local(): key_piece = lax.all_gather(key_rows, 'fsdp', axis=0, tiled=True)  32.8 us
    all_gather x1, waiting for transfers between devices, local(): value_piece = lax.all_gather(value_rows, 'fsdp', axis=0, tiled=True)  31.7 us
  transfers between devices with their start and end apart: 13, of which 9 were waited for; matrix products, arithmetic and copies ran while one was open for 32% of the time, Pallas kernels for 0%

commit v1 on v0

--- a/solution.py
+++ b/solution.py
@@ -80,8 +80,11 @@
         jnp.full((HEADS, tok_count), NEGATIVE, jnp.float32),
         jnp.zeros((HEADS, tok_count), jnp.float32),
     )
-    key_piece = lax.all_gather(key_rows, "fsdp", axis=0, tiled=True)
-    value_piece = lax.all_gather(value_rows, "fsdp", axis=0, tiled=True)
+    key_piece, value_piece = jnp.split(
+        lax.all_gather(jnp.concatenate([key_rows, value_rows], axis=1), "fsdp", axis=0, tiled=True),
+        [key_rows.shape[1]],
+        axis=1,
+    )
     block_rows, blocks = block_plan(key_piece.shape[0])
 
     def forward_advance(block_index, running_state):

time: 1010 us -> 1060 us (1.050)
  waiting for transfers between devices: 573 us -> 600 us
  local copies, waits for them, and re-layouts: 75.5 us -> 91.3 us
  matrix products: 220 us -> 235 us
    reduce_scatter x1, waiting for transfers between devices: 14.2 us -> 73.2 us  [local(): lax.psum_scatter(up_term, 'fsdp', scatter_dimension=0, tiled=True)]
    all_gather x1, waiting for transfers between devices: 15.2 us -> 0.02 us  [gather_feedforward(): lax.all_gather(up_weight, 'fsdp', axis=0, tiled=True)]
    all_gather x2 -> x3, waiting for transfers between devices: 64.5 us -> 49.5 us  [the longest x1 49.5 us: local(): lax.all_gather(jnp.concatenate([key_rows, value_rows], axis=1), 'fsdp', a...]
    dynamic_slice x0 -> x4, local copies, waits for them, and re-layouts: none -> 13.7 us  [the longest x2 7.86 us: forward_advance(): lax.dynamic_slice_in_dim(key_piece, offset, block_rows)]
    unnamed x78 -> x96, local copies, waits for them, and re-layouts: 25 us -> 12.2 us
  transfers between devices with their start and end apart: 13 -> 14, of which waited for: 9 -> 8; matrix products, arithmetic and copies ran while one was open for 32% -> 33% of each run, Pallas kernels for 0% -> 0%
where the time goes in v1:
time: 1060 us; the launch traced here: 1050 us
  waiting for transfers between devices  600 us (57%)
  matrix products  235 us (22%)
  local copies, waits for them, and re-layouts  91.3 us (9%)
  blocking collectives  68.3 us (6%)
  other arithmetic  43.3 us (4%)
  between operations  14.8 us (1%)
    psum x1, waiting for transfers between devices, local(): lax.psum((qkv_sum, out_sum, up_sum, down_sum), 'rep')  171 us
    reduce_scatter x1, waiting for transfers between devices, local(): lax.psum_scatter(down_term, 'fsdp', scatter_dimension=0, tiled=True)  120 us
    reduce_scatter x1, waiting for transfers between devices, local(): lax.psum_scatter(qkv_term, 'fsdp', scatter_dimension=0, tiled=True)  96.3 us
    reduce_scatter x1, waiting for transfers between devices, local(): lax.psum_scatter(up_term, 'fsdp', scatter_dimension=0, tiled=True)  73.2 us
    all_gather x1, waiting for transfers between devices, local(): lax.all_gather(jnp.concatenate([key_rows, value_rows], axis=1), 'fsdp', a...  49.5 us
    all_gather x1, waiting for transfers between devices, gather_attention(): lax.all_gather(qkv_weight, 'fsdp', axis=0, tiled=True)  48.7 us
    psum x1, blocking collectives, local(): lax.psum((bias_term, hidden_term, gain_term, shift_term), ('rep', 'fsdp'))  48.4 us
    all_gather x1, waiting for transfers between devices, gather_feedforward(): lax.all_gather(down_weight, 'fsdp', axis=0, tiled=True)  32.3 us
  transfers between devices with their start and end apart: 14, of which 8 were waited for; matrix products, arithmetic and copies ran while one was open for 33% of the time, Pallas kernels for 0%

profile of v1, /device:TPU:0, one launch (start us, length us, event | category | flops | bytes accessed | tf_op | source)
XLA Modules:
  0.0 1054.3 jit_solution(11069413270756224912)
XLA Ops:
  9.4 48.7 %all-gather.10.cloned.1.call-done = bf16[1024,3072]{1,0:T(8,128)(2,1)} async-done(((bf16[128,3072]{1,0:T(8,128)(2,1)}), bf16[1024,3072]{1,0:T(8,128)(2,1)}) %all-gather.10.cloned.1.call-update) | async-done | bytes 6291472 | tf_op jit(solution)/shard_map/all_gather | solution.py:23
  58.2 4.8 fusion.60
  72.9 49.5 %all-gather.12.cloned.1.call-done = bf16[2048,2048]{1,0:T(8,128)(2,1)} async-done(((bf16[256,2048]{1,0:T(8,128)(2,1)}), bf16[2048,2048]{1,0:T(8,128)(2,1)}) %all-gather.12.cloned.1.call-update) | async-done | bytes 8388624 | tf_op jit(solution)/shard_map/all_gather | solution.py:84
  122.5 6.0 fusion.73
  128.5 82.9 %while.48 = (s32[]{:T(128)}, f32[16,256,64]{1,2,0:T(8,128)}, f32[16,256]{1,0:T(8,128)S(1)}, f32[16,256]{1,0:T(8,128)S(1)}, s32[256]{0:T(256)S(1)}, /*index=5*/s3...) while((s32[]{:T(128)}, f32[16,256,64]{1,2,0:T(8,128)}, ...), condition=%wide.region_3.4_spmd.clone, body=%wide.region_0.3_spmd.clone.sunk | while | flops 1120948224 | bytes 75248824 | solution.py:113
  128.7 4.0 constant_dynamic-slice_fusion.13
  132.7 3.9 copy.81
  136.6 10.2 fusion.140
  146.9 9.3 fusion.141
  158.7 11.5 %fusion.143 = f32[16,256,64]{1,2,0:T(8,128)} fusion(bf16[1024,16,64]{0,2,1:T(8,128)(2,1)} %bitcast.185, f32[16,1024,256]{2,1,0:T(8,128)} %get-tuple-element.1004, f32[16,256]{1,0:T(8,128)S(1)} %select_maximum_fusion.2, pred[256,1024]{0,1:T(8,128)(4,1)S(1)} %broadcast_compare_fusion.6, f32[16,256,64]{1,2,0:T(8,128)} %get-tuple-element.1049, ...), kind=kOutput, calls=%fused_computation.9.clone.1 | convolution fusion | flops 554434560 | bytes 21266432 | tf_op jit(solution)/shard_map/while/body/eval_jaxpr/hqk,khd->hqd/dot_general | solution.py:105
  170.5 4.0 constant_dynamic-slice_fusion.13
  178.4 10.1 fusion.140
  188.5 9.3 fusion.141
  200.3 10.8 %fusion.143 = f32[16,256,64]{1,2,0:T(8,128)} fusion(bf16[1024,16,64]{0,2,1:T(8,128)(2,1)} %bitcast.185, f32[16,1024,256]{2,1,0:T(8,128)} %get-tuple-element.1004, f32[16,256]{1,0:T(8,128)S(1)} %select_maximum_fusion.2, pred[256,1024]{0,1:T(8,128)(4,1)S(1)} %broadcast_compare_fusion.6, f32[16,256,64]{1,2,0:T(8,128)} %get-tuple-element.1049, ...), kind=kOutput, calls=%fused_computation.9.clone.1 | convolution fusion | flops 554434560 | bytes 21266432 | tf_op jit(solution)/shard_map/while/body/eval_jaxpr/hqk,khd->hqd/dot_general | solution.py:105
  215.7 16.6 %multiply_convert_fusion.1 = (bf16[256,4096]{1,0:T(8,128)(2,1)}, f32[256,4096]{1,0:T(8,128)}, f32[256,4096]{1,0:T(8,128)}) fusion(f32[4096]{0:T(1024)S(1)} %copy-done.45, bf16[1024,4096]{1,0:T(8,128)(2,1)} %all-gather.16.cloned.1.call-done, f32[256,1024]{1,0:T(8,128)S(1)} %get-tuple-element.820, f32[1024]{0:T(1024)S(1)} %bitcast.206, ...), kind=kOutput, calls=%fused_computation.57 | convolution fusion | flops 2218000384 | bytes 19949568 | tf_op jit(solution)/shard_map/dot_general | solution.py:123
  232.3 32.3 %all-gather.18.cloned.1.call-done = bf16[4096,1024]{1,0:T(8,128)(2,1)} async-done(((bf16[512,1024]{1,0:T(8,128)(2,1)}), bf16[4096,1024]{1,0:T(8,128)(2,1)}) %all-gather.18.cloned.1.call-update) | async-done | bytes 8388624 | tf_op jit(solution)/shard_map/all_gather | solution.py:31
  264.6 6.5 fusion.78
  274.5 12.6 %convert_reduce_fusion = (f32[4096]{0:T(1024)}, bf16[256,4096]{1,0:T(8,128)(2,1)S(1)}) fusion(f32[256,4096]{1,0:T(8,128)} %get-tuple-element.795, f32[256,4096]{1,0:T(8,128)} %get-tuple-element.821, bf16[256,1024]{1,0:T(8,128)(2,1)S(1)} %get-tuple-element.789, bf16[4096,1024]{1,0:T(8,128)(2,1)} %all-gather.18.cloned.1.call-done), kind=kOutput, calls=%fused_computation.55 | convolution fusion | flops 2164256768 | bytes 19415040 | tf_op jit(solution)/shard_map/td,fd->tf/dot_general | solution.py:135
  297.1 9.9 fusion.67
  308.6 8.5 fusion.81
  325.5 10.6 %all_gather.47 = f32[16,2048]{1,0:T(8,128)} all-gather(f32[16,256]{1,0:T(8,128)S(1)} %fusion.56), channel_id=1, replica_groups=mesh['rep'=4,'fsdp'=8] {'fsdp'}, dimensions={1}, use_global_device_ids=true | all-gather | bytes 147456 | tf_op jit(solution)/shard_map/all_gather | solution.py:154
  336.2 9.3 all_gather.45
  345.5 66.8 %while.49 = (s32[]{:T(128)}, f32[16,256,64]{1,2,0:T(8,128)}, s32[256]{0:T(256)S(1)}, s32[2048]{0:T(1024)S(1)}, bf16[2048,1024]{1,0:T(8,128)(2,1)}, /*index=5*/bf...) while((s32[]{:T(128)}, f32[16,256,64]{1,2,0:T(8,128)}, ...), condition=%wide.region_13.14_spmd.clone, body=%wide.region_12.13_spmd.clone.sunk | while | flops 1636564992 | bytes 60339396 | solution.py:181
  345.5 4.7 constant_dynamic-slice_fusion.14
  353.2 8.1 fusion.149
  365.4 13.7 %fusion.150 = f32[16,256,64]{1,2,0:T(8,128)} fusion(bf16[1024,16,64]{0,2,1:T(8,128)(2,1)S(1)} %bitcast.178, f32[16,1024,256]{1,2,0:T(8,128)} %fusion.149, bf16[1024,16,64]{0,2,1:T(8,128)(2,1)} %bitcast.184, f32[16,256]{1,0:T(8,128)} %get-tuple-element.1156, f32[16,256]{1,0:T(8,128)} %get-tuple-element.1153, ...), kind=kOutput, calls=%fused_computation.24.clone.1 | convolution fusion | flops 1099431936 | bytes 23887872 | tf_op jit(solution)/shard_map/while/body/eval_jaxpr/hqk,khd->hqd/dot_general | solution.py:177
  379.1 4.7 constant_dynamic-slice_fusion.14
  386.7 8.4 fusion.149
  399.3 13.0 %fusion.150 = f32[16,256,64]{1,2,0:T(8,128)} fusion(bf16[1024,16,64]{0,2,1:T(8,128)(2,1)S(1)} %bitcast.178, f32[16,1024,256]{1,2,0:T(8,128)} %fusion.149, bf16[1024,16,64]{0,2,1:T(8,128)(2,1)} %bitcast.184, f32[16,256]{1,0:T(8,128)} %get-tuple-element.1156, f32[16,256]{1,0:T(8,128)} %get-tuple-element.1153, ...), kind=kOutput, calls=%fused_computation.24.clone.1 | convolution fusion | flops 1099431936 | bytes 23887872 | tf_op jit(solution)/shard_map/while/body/eval_jaxpr/hqk,khd->hqd/dot_general | solution.py:177
  414.4 5.9 all-gather.26.cloned.1.call-done
  420.3 91.1 %while.50 = (s32[]{:T(128)}, f32[16,256,64]{1,2,0:T(8,128)}, f32[16,256,64]{1,2,0:T(8,128)}, s32[2048]{0:T(1024)S(1)}, s32[256]{0:T(256)S(1)}, /*index=5*/bf16[2...) while((s32[]{:T(128)}, f32[16,256,64]{1,2,0:T(8,128)}, ...), condition=%wide.region_15.16_spmd.clone, body=%wide.region_14.15_spmd.clone.sunk | while | flops 2190737408 | bytes 84620544 | solution.py:219
  420.5 4.7 constant_dynamic-slice_fusion.15
  428.1 9.5 fusion.158
  437.7 4.0 copy.88
  441.9 9.9 fusion.160
  451.8 12.3 %fusion.159 = f32[16,256,64]{1,2,0:T(8,128)} fusion(bf16[1024,16,64]{0,2,1:T(8,128)(2,1)S(1)} %bitcast.180, f32[16,1024,256]{2,1,0:T(8,128)} %fusion.158, bf16[1024,16,64]{0,2,1:T(8,128)(2,1)} %bitcast.183, f32[16,1024]{1,0:T(8,128)S(1)} %get-tuple-element.1033, f32[16,1024]{1,0:T(8,128)S(1)} %get-tuple-element.1034, ...), kind=kOutput, calls=%fused_computation.40.clone.1 | convolution fusion | flops 1099431936 | bytes 23986176 | tf_op jit(solution)/shard_map/while/body/eval_jaxpr/hqk,qhd->hkd/dot_general | solution.py:214
  464.1 4.9 constant_dynamic-slice_fusion.15
  472.0 8.1 fusion.158
  480.1 4.0 copy.88
  484.3 12.3 %fusion.160 = f32[16,256,64]{1,2,0:T(8,128)} fusion(bf16[1024,16,64]{0,2,1:T(8,128)(2,1)} %bitcast.182, f32[16,1024,256]{2,1,0:T(8,128)} %fusion.158, f32[16,1024]{1,0:T(8,128)S(1)} %get-tuple-element.1034, pred[1024,256]{1,0:T(8,128)(4,1)S(1)} %broadcast_compare_fusion.8, f32[16,256,64]{1,2,0:T(8,128)} %get-tuple-element.1091, pred[]{:T(512)S(6)} %compare.11), kind=kOutput, calls=%fused_computation.39.clone.1 | convolution fusion | flops 554172416 | bytes 21299200 | tf_op jit(solution)/shard_map/while/body/eval_jaxpr/hqk,qhd->hkd/dot_general | solution.py:204
  496.7 14.8 %fusion.159 = f32[16,256,64]{1,2,0:T(8,128)} fusion(bf16[1024,16,64]{0,2,1:T(8,128)(2,1)S(1)} %bitcast.180, f32[16,1024,256]{2,1,0:T(8,128)} %fusion.158, bf16[1024,16,64]{0,2,1:T(8,128)(2,1)} %bitcast.183, f32[16,1024]{1,0:T(8,128)S(1)} %get-tuple-element.1033, f32[16,1024]{1,0:T(8,128)S(1)} %get-tuple-element.1034, ...), kind=kOutput, calls=%fused_computation.40.clone.1 | convolution fusion | flops 1099431936 | bytes 23986176 | tf_op jit(solution)/shard_map/while/body/eval_jaxpr/hqk,qhd->hkd/dot_general | solution.py:214
  514.0 7.4 convolution_bitcast_fusion
  521.7 73.2 %reduce-scatter.9.cloned.1.call-done = f32[128,4096]{1,0:T(8,128)} async-done(((f32[1024,4096]{1,0:T(8,128)}), f32[128,4096]{1,0:T(8,128)}) %reduce-scatter.9.cloned.1.call-update) | async-done | bytes 2097168 | tf_op jit(solution)/shard_map/reduce_scatter | solution.py:242
  594.9 119.8 %reduce-scatter.11.cloned.1.call-done = f32[512,1024]{1,0:T(8,128)} async-done(((f32[4096,1024]{1,0:T(8,128)}), f32[512,1024]{1,0:T(8,128)}) %reduce-scatter.11.cloned.1.call-update) | async-done | bytes 2097168 | tf_op jit(solution)/shard_map/reduce_scatter | solution.py:243
  714.7 96.3 %reduce-scatter.5.cloned.1.call-done = f32[128,3072]{0,1:T(8,128)} async-done(((f32[1024,3072]{0,1:T(8,128)}), f32[128,3072]{0,1:T(8,128)}) %reduce-scatter.5.cloned.1.call-update) | async-done | bytes 1572880 | tf_op jit(solution)/shard_map/reduce_scatter | solution.py:246
  811.4 48.4 %all-reduce = (f32[4,1024]{1,0:T(4,128)S(1)}, f32[4096]{0:T(1024)S(1)}, f32[2,1024]{1,0:T(2,128)S(1)}, f32[2,1024]{1,0:T(2,128)S(1)}) all-reduce(f32[4,1024]{1,0:T(4,128)S(1)} %pad_maximum_fusion.4, f32[4096]{0:T(1024)S(1)} %copy-done.37, f32[2,1024]{1,0:T(2,128)S(1)} %get-tuple-element.826, ...), channel_id=1, replica_groups=mesh['rep'=4,'fsdp'=8] {'rep','fsdp'}, use_global_device_ids=true, to_apply=%region_28.29 | all-reduce | flops 12288 | bytes 98304 | tf_op jit(solution)/shard_map/psum | solution.py:238
  862.2 5.6 fusion.51
  867.8 170.8 %all-reduce.4.cloned.1.call-done = (f32[128,3072]{0,1:T(8,128)}, f32[128,1024]{1,0:T(8,128)}, f32[128,4096]{1,0:T(8,128)}, f32[512,1024]{1,0:T(8,128)}) async-done(((f32[128,3072]{0,1:T(8,128)}, f32[128,1024]{1,0:T(8,128)}, f32[128,4096]{1,0:T(8,128)}, f32[512,1024]{1,0:T(8,128)}), (f32[128,3072]{0,1:T(8,128)}, f32[128,1024]{1,0:T(8,128)}, f32[128,4096]{1,0:T(8,128)}, ...) | async-done | bytes 6291472 | tf_op jit(solution)/shard_map/psum | solution.py:249
  (222 shorter events, 85.9 us)
Async XLA Ops:
  7.2 51.0 %all-gather.10.cloned.1.call-start = ((), (), s32[]{:S(2)}) async-start(), calls=%async_computation.4 | async-start | bytes 7077888 | tf_op jit(solution)/shard_map/all_gather | solution.py:23
  7.9 114.5 %all-gather.12.cloned.1.call-start = ((), (), s32[]{:S(2)}) async-start(), calls=%async_computation.5 | async-start | bytes 9437184 | tf_op jit(solution)/shard_map/all_gather | solution.py:84
  64.6 5.2 copy-start.3
  64.6 6.6 copy-start.26
  64.7 6.6 copy-start.38
  64.7 7.2 copy-start.39
  66.7 6.0 copy-start.9
  67.9 145.0 %all-gather.14.cloned.1.call-start = ((), (), s32[]{:S(2)}) async-start(), calls=%async_computation.6 | async-start | bytes 2359296 | tf_op jit(solution)/shard_map/all_gather | solution.py:24
  68.6 147.0 %all-gather.16.cloned.1.call-start = ((), (), s32[]{:S(2)}) async-start(), calls=%async_computation.7 | async-start | bytes 9437184 | tf_op jit(solution)/shard_map/all_gather | solution.py:30
  69.2 195.4 %all-gather.18.cloned.1.call-start = ((), (), s32[]{:S(2)}) async-start(), calls=%async_computation.8 | async-start | bytes 9437184 | tf_op jit(solution)/shard_map/all_gather | solution.py:31
  69.8 275.7 %all-gather.22.cloned.1.call-start = ((), (), s32[]{:S(2)}) async-start(), calls=%async_computation.10 | async-start | bytes 4718592 | tf_op jit(solution)/shard_map/all_gather | solution.py:157
  70.4 275.1 %all-gather.20.cloned.1.call-start = ((), (), s32[]{:S(2)}) async-start(), calls=%async_computation.9 | async-start | bytes 4718592 | tf_op jit(solution)/shard_map/all_gather | solution.py:156
  71.1 343.2 %all-gather.24.cloned.1.call-start = ((), (), s32[]{:S(2)}) async-start(), calls=%async_computation.11 | async-start | bytes 4718592 | tf_op jit(solution)/shard_map/all_gather | solution.py:186
  72.7 347.6 %all-gather.26.cloned.1.call-start = ((), (), s32[]{:S(2)}) async-start(), calls=%async_computation.12 | async-start | bytes 4718592 | tf_op jit(solution)/shard_map/all_gather | solution.py:187
  128.5 84.5 %copy-start.15 = (bf16[1,256,1024]{2,1,0:T(8,128)(2,1)S(1)}, bf16[1,256,1024]{2,1,0:T(8,128)(2,1)}, u32[]{:S(2)}) copy-start(bf16[1,256,1024]{2,1,0:T(8,128)(2,1)} %param.17) | copy-start | bytes 1572868
  211.4 20.9 %copy-start = (bf16[256,16,64]{0,2,1:T(8,128)(2,1)}, bf16[256,16,64]{0,2,1:T(8,128)(2,1)S(1)}, u32[]{:S(2)}) copy-start(bf16[256,16,64]{0,2,1:T(8,128)(2,1)S(1)} %get-tuple-element.1194) | copy-start | bytes 1572868
  211.4 20.9 %copy-start.28 = (s32[256]{0:T(256)}, s32[256]{0:T(256)S(1)}, u32[]{:S(2)}) copy-start(s32[256]{0:T(256)S(1)} %get-tuple-element.1229) | copy-start | bytes 3076
  215.7 48.9 %copy-start.42 = (f32[1,1024]{1,0:T(1,128)S(1)}, f32[1,1024]{1,0:T(1,128)}, u32[]{:S(2)}) copy-start(f32[1,1024]{1,0:T(1,128)} %get-tuple-element.811) | copy-start | bytes 12292
  264.6 6.8 copy-start.7
  264.6 6.8 copy-start.32
  264.6 7.9 copy-start.33
  272.5 14.7 %slice-start = ((s8[8388608]{0:T(1024)(128)(4,1)}), s8[4194304]{0:T(1024)(128)(4,1)S(1)}, s32[]{:S(2)}) async-start(s8[8388608]{0:T(1024)(128)(4,1)} %bitcast.222), calls=%async_computation.18 | async-start | bytes 8388608
  274.5 12.6 %slice-start.1 = ((s8[8388608]{0:T(1024)(128)(4,1)}), s8[4194304]{0:T(1024)(128)(4,1)S(1)}, s32[]{:S(2)}) async-start(s8[8388608]{0:T(1024)(128)(4,1)} %bitcast.222), calls=%async_computation.19 | async-start | bytes 8388608
  290.9 6.2 copy-start.43
  294.2 227.5 %reduce-scatter.7.cloned.1.call-start = ((), (), s32[]{:S(2)}) async-start(), calls=%async_computation.14 | async-start | bytes 4718592 | tf_op jit(solution)/shard_map/reduce_scatter | solution.py:247
  297.1 297.8 %reduce-scatter.9.cloned.1.call-start = ((), (), s32[]{:S(2)}) async-start(), calls=%async_computation.15 | async-start | bytes 18874368 | tf_op jit(solution)/shard_map/reduce_scatter | solution.py:242
  307.0 407.7 %reduce-scatter.11.cloned.1.call-start = ((), (), s32[]{:S(2)}) async-start(), calls=%async_computation.16 | async-start | bytes 18874368 | tf_op jit(solution)/shard_map/reduce_scatter | solution.py:243
  317.1 493.9 %reduce-scatter.5.cloned.1.call-start = ((), (), s32[]{:S(2)}) async-start(), calls=%async_computation.13 | async-start | bytes 14155776 | tf_op jit(solution)/shard_map/reduce_scatter | solution.py:246
  319.1 26.4 %copy-start.27 = (s32[1,2048]{1,0:T(1,128)S(1)}, s32[1,2048]{1,0:T(1,128)}, u32[]{:S(2)}) copy-start(s32[1,2048]{1,0:T(1,128)} %param.18) | copy-start | bytes 24580
  319.1 26.4 %copy-start.29 = (s32[256]{0:T(256)S(1)}, s32[256]{0:T(256)}, u32[]{:S(2)}) copy-start(s32[256]{0:T(256)} %copy-done.28) | copy-start | bytes 3076
  319.3 6.0 copy-start.12
  325.5 20.0 %copy-start.30 = (f32[16,256]{1,0:T(8,128)}, f32[16,256]{1,0:T(8,128)S(1)}, u32[]{:S(2)}) copy-start(f32[16,256]{1,0:T(8,128)S(1)} %fusion.56) | copy-start | bytes 49156
  336.2 9.3 copy-start.31
  345.5 74.8 %copy-start.23 = (f32[16,2048]{1,0:T(8,128)S(1)}, f32[16,2048]{1,0:T(8,128)}, u32[]{:S(2)}) copy-start(f32[16,2048]{1,0:T(8,128)} %all_gather.47) | copy-start | bytes 393220
  420.3 93.7 %copy-start.16 = (bf16[1,256,1024]{2,1,0:T(8,128)(2,1)S(1)}, bf16[1,256,1024]{2,1,0:T(8,128)(2,1)}, u32[]{:S(2)}) copy-start(bf16[1,256,1024]{2,1,0:T(8,128)(2,1)} %param.17) | copy-start | bytes 1572868
  521.5 289.6 %copy-start.8 = (bf16[1,256,1024]{2,1,0:T(8,128)(2,1)S(1)}, bf16[1,256,1024]{2,1,0:T(8,128)(2,1)}, u32[]{:S(2)}) copy-start(bf16[1,256,1024]{2,1,0:T(8,128)(2,1)} %param.27) | copy-start | bytes 1572868
  521.5 289.7 %copy-start.34 = (f32[1024]{0:T(1024)S(1)}, f32[1024]{0:T(1024)}, u32[]{:S(2)}) copy-start(f32[1024]{0:T(1024)} %get-tuple-element.707) | copy-start | bytes 12292
  521.5 289.7 %copy-start.40 = (f32[1024]{0:T(1024)S(1)}, f32[1024]{0:T(1024)}, u32[]{:S(2)}) copy-start(f32[1024]{0:T(1024)} %get-tuple-element.705) | copy-start | bytes 12292
  521.5 289.7 %copy-start.41 = (f32[1024]{0:T(1024)S(1)}, f32[1024]{0:T(1024)}, u32[]{:S(2)}) copy-start(f32[1024]{0:T(1024)} %get-tuple-element.709) | copy-start | bytes 12292
  521.5 289.8 %copy-start.35 = (f32[1024]{0:T(1024)S(1)}, f32[1024]{0:T(1024)}, u32[]{:S(2)}) copy-start(f32[1024]{0:T(1024)} %get-tuple-element.788) | copy-start | bytes 12292
  521.5 289.8 %copy-start.36 = (f32[1024]{0:T(1024)S(1)}, f32[1024]{0:T(1024)}, u32[]{:S(2)}) copy-start(f32[1024]{0:T(1024)} %get-tuple-element.786) | copy-start | bytes 12292
  521.5 289.8 %copy-start.37 = (f32[4096]{0:T(1024)S(1)}, f32[4096]{0:T(1024)}, u32[]{:S(2)}) copy-start(f32[4096]{0:T(1024)} %get-tuple-element.780) | copy-start | bytes 49156
  521.5 340.7 %copy-start.11 = (f32[256,1024]{1,0:T(8,128)S(1)}, f32[256,1024]{1,0:T(8,128)}, u32[]{:S(2)}) copy-start(f32[256,1024]{1,0:T(8,128)} %copy-done.10) | copy-start | bytes 3145732
  521.6 340.7 %copy-start.17 = (bf16[16,256,64]{1,2,0:T(8,128)(2,1)S(1)}, bf16[16,256,64]{1,2,0:T(8,128)(2,1)}, u32[]{:S(2)}) copy-start(bf16[16,256,64]{1,2,0:T(8,128)(2,1)} %get-tuple-element.783) | copy-start | bytes 1572868
  521.6 340.7 %copy-start.21 = (bf16[16,256,64]{1,2,0:T(8,128)(2,1)S(1)}, bf16[16,256,64]{1,2,0:T(8,128)(2,1)}, u32[]{:S(2)}) copy-start(bf16[16,256,64]{1,2,0:T(8,128)(2,1)} %copy-done.20) | copy-start | bytes 1572868
  521.6 340.6 %copy-start.44 = (f32[256]{0:T(256)S(1)}, f32[256]{0:T(256)}, u32[]{:S(2)}) copy-start(f32[256]{0:T(256)} %copy-done.43) | copy-start | bytes 3076
  521.6 517.0 %all-reduce.4.cloned.1.call-start = ((), (), s32[]{:S(2)}) async-start(), calls=%async_computation.17 | async-start | bytes 12582912 | tf_op jit(solution)/shard_map/psum | solution.py:249
  1041.7 5.0 copy-start.25
  (16 other events, 40.5 us)
Sparse Core Ops, SparseCore 0:
  9.9 48.2 all-gather.9
  68.0 54.3 all-gather.11
  124.3 27.8 all-gather.13
  154.0 54.3 all-gather.15
  210.2 54.3 all-gather.17
  266.3 36.7 all-gather.21
  305.6 37.3 all-gather.19
  344.8 36.7 all-gather.23
  383.5 36.7 all-gather.25
  423.5 51.3 reduce-scatter.6
  478.9 115.9 reduce-scatter.8
  598.7 115.9 reduce-scatter.10
  718.6 92.3 reduce-scatter.4
  813.7 224.8 all-reduce.3
